TPU v7x, 256 devices: a whole 4x4x8 slice. The times are simulated.
256 devices in a mesh: row: 16 (over x, y_hi, core), col: 16 (over z, y_lo).
Axes of the slice: x: 4, y: 4 (y_hi: 2, y_lo: 2; y = y_hi * 2 + y_lo), z: 8, core: 2. Of those that a mesh axis runs over, the one named last changes fastest.
Arguments:
- p_cols: int32 [256, 64], P('row', 'col'), may hold values from -1 to 15, as said below
- p_data: float32 [16384, 4096], P('row', 'col'), may hold values from -1.5 to 1.5
Outputs:
- product: float32 [16384, 16384], P('row', 'col')
Inputs may be any that keep to these rules, and one draw needn't show every extreme that they name: `p_cols`: in each column tile, each block row has 1 to 4 used slots, the used ones first, with distinct columns; the first block row of each device's rows has all 4 used.
All inputs are finite; a program needn't handle non-finite values.
Results may differ from a plain program's by a relative error of at most 0.0003.
Values sent between devices are 32-bit elements; how exact they have to be, the bound alone decides.
A program may use at most 192 MiB of HBM per device.

v0:
```python
import functools

import jax
import jax.numpy as jnp
from jax import lax
from jax.experimental import pallas as pl
from jax.experimental.pallas import tpu as pltpu
from jax.sharding import PartitionSpec as P

BS = 64
STEPS = 4
PIECES = 4
PIECE_ROWS = 1024 // PIECES
PIECE_BLOCKS = PIECE_ROWS // BS
COLS = PIECES
ALL = (COLS,) + tuple(range(PIECES))
MESH = pl.DeviceIdType.MESH


def kernel(
    cols_hbm, data_hbm, out_hbm,
    own, own_cols, left, left_cols, right, right_cols, high, low, out, left_at, right_at,
    load_sem, keep_sem, send_sem, left_sem, right_sem, at_sem, out_sem,
):
    row, col = lax.axis_index("row"), lax.axis_index("col")
    q, core = row // 2, row % 2
    half = q % 2
    z, y = col // 2, col % 2
    odd = z % 2 == 1

    def at(q_new, z_new, y_new, core_new):
        return (2 * ((q_new + 32) % 8) + core_new, 2 * ((z_new + 32) % 8) + y_new)

    depth = q + core
    land = jnp.where((depth >= 5) & (depth <= 7) | (depth >= 3) & (depth <= 4) & (core == 1), 1, 0)
    skew = depth + land
    left_own = skew % 8 == 0
    lane = 2 * land - 1

    def near_slot(index):
        return 2 * index + core

    def cross_slot(index):
        return 2 * index + 1 - core

    def cross_at(y_here):
        free = jnp.where(q <= 2, 1, jnp.where(q >= 4, 0, core))
        return jnp.where(y_here == core, free, core)

    crossed = cross_at(y)
    pass_lane = 2 * crossed - 1
    cross_as = cross_at(1 - y)
    cross_of = 1 - y + cross_as - core

    first = jnp.where(odd, 1, jnp.where(z < 4, 0, 2))
    right_own = (z + first) % 8 == 0
    second = jnp.where(odd, 2 - 2 * half, 2 - first)
    third = 3 - first - second

    def own_slot(index):
        return (2 * index - y + 5) % 5

    def shared_slot(index):
        return 2 * (index + core) + 1 - 2 * core - y

    hop = 1 - 2 * half
    send1_to = q + jnp.where(odd, hop, 2 * first - 2)
    send1_as = jnp.where(odd, 1 - hop, 2 - first)
    send2_of = jnp.where(odd, second, 2 - 2 * half)
    send2_to = q + jnp.where(odd, 2 * hop, hop)
    send2_as = jnp.where(odd, third, 1)

    barrier = pltpu.get_barrier_semaphore()

    def greet(device):
        pl.semaphore_signal(barrier, inc=1, device_id=device, device_id_type=MESH)

    @pl.when(jnp.logical_not(left_own))
    def _():
        greet(at(q, z + skew, y, core))

    greet(at(q, z - lane, y, core))
    greet(at(q, z, 1 - y, core))
    greet(at(q, z - pass_lane, y, core))

    @pl.when(jnp.logical_not(right_own))
    def _():
        greet(at(q + z + first, z, y, core))

    greet(at(q + jnp.where(odd, hop, 2 - 2 * first), z, y, core))
    greet(at(q + jnp.where(odd, -2 * hop, hop), z, y, core))
    greet(at(q, z, y, 1 - core))

    load = pltpu.make_async_copy(data_hbm, own, load_sem.at[0])
    load_cols = pltpu.make_async_copy(cols_hbm, own_cols, load_sem.at[1])
    load.start()
    load_cols.start()
    load.wait()
    load_cols.wait()
    pl.semaphore_wait(barrier, 8 - left_own.astype(jnp.int32) - right_own.astype(jnp.int32))

    def rows(piece):
        return pl.ds(piece * PIECE_ROWS, PIECE_ROWS)

    def own_part(piece):
        return own_cols if piece == COLS else own.at[rows(piece)]

    def left_part(slot, piece):
        return left_cols.at[slot] if piece == COLS else left.at[slot, rows(piece)]

    def right_part(slot, piece):
        return right_cols.at[slot] if piece == COLS else right.at[slot, rows(piece)]

    def move(source, target, kind, piece, sem, device):
        return pltpu.make_async_remote_copy(
            src_ref=source,
            dst_ref=target,
            send_sem=send_sem.at[kind, piece],
            recv_sem=sem,
            device_id=device,
            device_id_type=MESH,
        )

    def to_left(source, slot, kind, piece, device):
        return move(source, left_part(slot, piece), kind, piece, left_sem.at[slot, piece], device)

    def to_right(source, slot, kind, piece, device):
        return move(source, right_part(slot, piece), kind, piece, right_sem.at[slot, piece], device)

    def left_skew(piece):
        return to_left(own_part(piece), near_slot(land), 0, piece, at(q, z - skew, y, core))

    def left_next(piece):
        return to_left(left_part(near_slot(land), piece), near_slot(1 - land), 1, piece, at(q, z + lane, y, core))

    def left_cross(piece):
        return to_left(left_part(near_slot(cross_of), piece), cross_slot(cross_as), 2, piece, at(q, z, 1 - y, core))

    def left_pass(piece):
        source = left_part(cross_slot(crossed), piece)
        return to_left(source, cross_slot(1 - crossed), 3, piece, at(q, z + pass_lane, y, core))

    def right_skew(piece):
        return to_right(own_part(piece), own_slot(first), 4, piece, at(q - z - first, z, y, core))

    def right_send1(piece):
        return to_right(right_part(own_slot(first), piece), own_slot(send1_as), 5, piece, at(send1_to, z, y, core))

    def right_send2(piece):
        return to_right(right_part(own_slot(send2_of), piece), own_slot(send2_as), 6, piece, at(send2_to, z, y, core))

    def right_share(index, kind, piece):
        slot = 2 * index - 1 + 2 * core - y
        return to_right(right_part(own_slot(index), piece), slot, kind, piece, at(q, z, y, 1 - core))

    def left_here(slot, piece):
        to_left(left_part(slot, piece), slot, 0, piece, at(q, z, 1 - y, core)).wait_recv()

    def right_here(slot, piece):
        to_right(right_part(slot, piece), slot, 0, piece, at(q, z, 1 - y, core)).wait_recv()

    def keep_left(piece):
        return pltpu.make_async_copy(own_part(piece), left_part(near_slot(land), piece), keep_sem.at[0, piece])

    def keep_right(piece):
        return pltpu.make_async_copy(own_part(piece), right_part(own_slot(first), piece), keep_sem.at[1, piece])

    def shares(index):
        return index != 2 * core

    side = lax.broadcasted_iota(jnp.int32, (BS, 128), 1) // BS

    def spread(slot, piece):
        def one(index, carry):
            inner = piece * PIECE_BLOCKS + index
            here = pl.ds(pl.multiple_of(inner * BS, BS), BS)
            block = right[slot, here, :]
            top = block.astype(jnp.bfloat16)
            rest = (block - top.astype(jnp.float32)).astype(jnp.bfloat16)
            targets = [right_at[slot, inner, place] for place in range(4)]
            for value, kept in ((top, high), (rest, low)):
                doubled = []
                for pair in range(2):
                    both = value[:, pair * 128 : pair * 128 + 128]
                    even, uneven = both[:, :BS], both[:, BS:]
                    doubled.append(jnp.concatenate([even, even], axis=1))
                    doubled.append(jnp.concatenate([uneven, uneven], axis=1))
                for group in range(8):
                    spot = side + 2 * group
                    result = jnp.zeros((BS, 128), jnp.bfloat16)
                    for place in range(4):
                        result = jnp.where(spot == targets[place], doubled[place], result)
                    kept[slot, inner, :, group * 128 : group * 128 + 128] = result
            return carry

        lax.fori_loop(0, PIECE_BLOCKS, one, 0)

    def right_ready(slot, piece):
        if piece == COLS:
            copy = pltpu.make_async_copy(right_cols.at[slot], right_at.at[slot], at_sem)
            copy.start()
            copy.wait()
        else:
            spread(slot, piece)

    def own_ready(index, piece):
        @pl.when(own_slot(index) < 4)
        def _():
            right_ready(own_slot(index), piece)

    def products(piece):
        def one(index, carry):
            block_row = piece * PIECE_BLOCKS + index
            here = pl.ds(pl.multiple_of(block_row * BS, BS), BS)
            place = lax.broadcasted_iota(jnp.int32, (BS, 256), 1) // BS
            tops, rests, starts = [], [], []
            for step in range(STEPS):
                used = jnp.zeros((BS, 256), jnp.bool_)
                for slot in range(4):
                    inner = left_at[step, block_row, slot]
                    used = used | (place == jnp.where(inner >= 0, slot, -1))
                    starts.append((step, jnp.maximum(inner, 0)))
                block = jnp.where(used, left[step, here, :], 0.0)
                top = block.astype(jnp.bfloat16)
                tops.append(top)
                rests.append((block - top.astype(jnp.float32)).astype(jnp.bfloat16))
            top = jnp.concatenate(tops, axis=1)
            both = jnp.concatenate([top, jnp.concatenate(rests, axis=1)], axis=0)
            for quarter in range(4):
                lanes = slice(quarter * 256, quarter * 256 + 256)
                right_top = jnp.concatenate([high[step, start, :, lanes] for step, start in starts], axis=0)
                right_rest = jnp.concatenate([low[step, start, :, lanes] for step, start in starts], axis=0)
                main = jnp.dot(both, right_top, preferred_element_type=jnp.float32)
                extra = jnp.dot(top, right_rest, preferred_element_type=jnp.float32)
                out[here, lanes] = main[:BS] + main[BS:] + extra
            return carry

        lax.fori_loop(0, PIECE_BLOCKS, one, 0)
        write(piece).start()

    def write(piece):
        return pltpu.make_async_copy(out.at[rows(piece)], out_hbm.at[rows(piece)], out_sem.at[piece])

    for piece in ALL:
        @pl.when(left_own)
        def _():
            keep_left(piece).start()

        @pl.when(jnp.logical_not(left_own))
        def _():
            left_skew(piece).start()

        @pl.when(right_own)
        def _():
            keep_right(piece).start()

        @pl.when(jnp.logical_not(right_own))
        def _():
            right_skew(piece).start()

    def right_first(piece):
        @pl.when(right_own)
        def _():
            keep_right(piece).wait()

        @pl.when(jnp.logical_not(right_own))
        def _():
            right_here(own_slot(first), piece)

        right_send1(piece).start()

        @pl.when(shares(first))
        def _():
            right_share(first, 7, piece).start()

    def right_second(piece):
        right_here(own_slot(second), piece)
        right_send2(piece).start()

        @pl.when(shares(second))
        def _():
            right_share(second, 8, piece).start()

    def right_third(piece):
        right_here(own_slot(third), piece)

        @pl.when(shares(third))
        def _():
            right_share(third, 9, piece).start()

    def left_first(piece):
        @pl.when(left_own)
        def _():
            keep_left(piece).wait()

        @pl.when(jnp.logical_not(left_own))
        def _():
            left_here(near_slot(land), piece)

        left_next(piece).start()

        @pl.when(cross_of == land)
        def _():
            left_cross(piece).start()

    def left_second(piece):
        left_here(near_slot(1 - land), piece)

        @pl.when(cross_of != land)
        def _():
            left_cross(piece).start()

    def left_third(piece):
        left_here(cross_slot(crossed), piece)
        left_pass(piece).start()

    def left_last(piece):
        left_here(cross_slot(1 - crossed), piece)

    def lagged(stages):
        for turn in range(len(ALL) + len(stages) - 1):
            for lag, stage in enumerate(stages):
                if 0 <= turn - lag < len(ALL):
                    stage(ALL[turn - lag])

    def landed(piece):
        right_first(piece)
        left_first(piece)
        own_ready(first, piece)

    def followed(piece):
        right_second(piece)
        own_ready(second, piece)

    def finished(piece):
        right_third(piece)
        left_second(piece)
        own_ready(third, piece)

    def shared(piece):
        left_third(piece)
        for index in range(2):
            right_here(shared_slot(index), piece)
            right_ready(shared_slot(index), piece)

    lagged((landed, followed))
    lagged((finished, shared))
    for piece in ALL:
        left_last(piece)
        if piece == COLS:
            copy = pltpu.make_async_copy(left_cols, left_at, at_sem)
            copy.start()
            copy.wait()
        else:
            products(piece)

    for piece in ALL:
        @pl.when(jnp.logical_not(left_own))
        def _():
            left_skew(piece).wait_send()

        @pl.when(jnp.logical_not(right_own))
        def _():
            right_skew(piece).wait_send()

        left_next(piece).wait_send()
        left_cross(piece).wait_send()
        left_pass(piece).wait_send()
        right_send1(piece).wait_send()
        right_send2(piece).wait_send()
        for index, kind in ((first, 7), (second, 8), (third, 9)):
            @pl.when(shares(index))
            def _():
                right_share(index, kind, piece).wait_send()

        if piece != COLS:
            write(piece).wait()


def local(p_cols, p_data):
    count = len(ALL)
    return pl.pallas_call(
        kernel,
        out_shape=jax.ShapeDtypeStruct((1024, 1024), jnp.float32),
        in_specs=[pl.BlockSpec(memory_space=pl.ANY)] * 2,
        out_specs=pl.BlockSpec(memory_space=pl.ANY),
        scratch_shapes=[
            pltpu.VMEM((1024, 256), jnp.float32),
            pltpu.VMEM((16, 4), jnp.int32),
            pltpu.VMEM((4, 1024, 256), jnp.float32),
            pltpu.VMEM((4, 16, 4), jnp.int32),
            pltpu.VMEM((5, 1024, 256), jnp.float32),
            pltpu.VMEM((5, 16, 4), jnp.int32),
            pltpu.VMEM((STEPS, 16, BS, 1024), jnp.bfloat16),
            pltpu.VMEM((STEPS, 16, BS, 1024), jnp.bfloat16),
            pltpu.VMEM((1024, 1024), jnp.float32),
            pltpu.SMEM((4, 16, 4), jnp.int32),
            pltpu.SMEM((4, 16, 4), jnp.int32),
            pltpu.SemaphoreType.DMA((2,)),
            pltpu.SemaphoreType.DMA((2, count)),
            pltpu.SemaphoreType.DMA((10, count)),
            pltpu.SemaphoreType.DMA((4, count)),
            pltpu.SemaphoreType.DMA((5, count)),
            pltpu.SemaphoreType.DMA,
            pltpu.SemaphoreType.DMA((PIECES,)),
        ],
        compiler_params=pltpu.CompilerParams(collective_id=0, has_side_effects=True),
        name="window_square",
    )(p_cols, p_data)


def solution(mesh):
    return jax.shard_map(
        local, mesh=mesh, in_specs=(P("row", "col"), P("row", "col")), out_specs=P("row", "col"), check_vma=False
    )
```

profile of v0, /device:TPU:12, one launch (start us, length us, event | category | flops | bytes accessed | tf_op | source)
XLA Modules:
  0.0 113.2 jit_solution(5688378713711225735)
XLA Ops:
  0.0 1.4 %copy.3.cols_hbm = s32[16,4]{1,0:T(8,128)} copy(s32[16,4]{0,1:T(4,128)} %param.2) | data formatting | bytes 512 | tf_op args[0]
  1.4 107.0 %window_square.1 = f32[1024,1024]{1,0:T(8,128)} custom-call(s32[16,4]{1,0:T(8,128)} %copy.3.cols_hbm, f32[1024,256]{1,0:T(8,128)} %data_hbm.1), custom_call_target="tpu_custom_call" | custom-call | tf_op jit(solution)/shard_map/window_square/pallas_call | solution.py:382
  108.4 4.8 %copy.5 = f32[1024,1024]{1,0:T(8,128)} copy(f32[1024,1024]{1,0:T(8,128)} %window_square.1) | data formatting | bytes 8388608
where the time goes:
time: 113 us
  Pallas kernels  107 us (95%)
  local copies, waits for them, and re-layouts  6.14 us (5%)
    pallas_call x1, Pallas kernels, local(): pl.pallas_call(kernel, out_shape=jax.ShapeDtypeStruct((1024, 1024), jnp.f...  107 us
    unnamed x2, local copies, waits for them, and re-layouts  6.14 us

commit v1 on v0

--- a/solution.py
+++ b/solution.py
@@ -9,18 +9,24 @@
 
 BS = 64
 STEPS = 4
-PIECES = 4
+PIECES = 8
 PIECE_ROWS = 1024 // PIECES
 PIECE_BLOCKS = PIECE_ROWS // BS
 COLS = PIECES
+LEFT_AHEAD = 3
+RIGHT_AHEAD = 3
+RIGHT_PACE = 0.6
+RIGHT_LAG = 1.4
+LEFT_LAG = 2.0
+END_LAG = 2.0
 ALL = (COLS,) + tuple(range(PIECES))
 MESH = pl.DeviceIdType.MESH
 
 
 def kernel(
     cols_hbm, data_hbm, out_hbm,
-    own, own_cols, left, left_cols, right, right_cols, high, low, out, left_at, right_at,
-    load_sem, keep_sem, send_sem, left_sem, right_sem, at_sem, out_sem,
+    own, own_cols, left, left_cols, right, right_cols, relay, high, low, out, left_at, right_at,
+    load_sem, keep_sem, send_sem, left_sem, right_sem, relay_sem, at_sem, out_sem,
 ):
     row, col = lax.axis_index("row"), lax.axis_index("col")
     q, core = row // 2, row % 2
@@ -32,10 +38,26 @@
         return (2 * ((q_new + 32) % 8) + core_new, 2 * ((z_new + 32) % 8) + y_new)
 
     depth = q + core
-    land = jnp.where((depth >= 5) & (depth <= 7) | (depth >= 3) & (depth <= 4) & (core == 1), 1, 0)
+    land = jnp.where((depth >= 5) & (depth <= 7) | (q == 3) & (core == 1) | (q == 4) & (core == 0), 1, 0)
     skew = depth + land
     left_own = skew % 8 == 0
     lane = 2 * land - 1
+    some = (q == 1) & (core == 1) | (q == 5) & (core == 0)
+    most = (q == 2) & (core == 1) | (q == 4) & (core == 0)
+    relays = some | most
+    long_lane = -lane
+    long_way = jnp.where(land == 0, 7 - depth, depth)
+
+    def takes_long(piece):
+        if piece == COLS or piece % 4 == 3:
+            return q < 0
+        return relays if piece % 4 == 0 else most
+
+    def land_of(piece):
+        return jnp.where(takes_long(piece), 1 - land, land)
+
+    def lane_of(piece):
+        return jnp.where(takes_long(piece), long_lane, lane)
 
     def near_slot(index):
         return 2 * index + core
@@ -44,7 +66,7 @@
         return 2 * index + 1 - core
 
     def cross_at(y_here):
-        free = jnp.where(q <= 2, 1, jnp.where(q >= 4, 0, core))
+        free = jnp.where(q <= 1, 1, jnp.where(q >= 5, 0, core))
         return jnp.where(y_here == core, free, core)
 
     crossed = cross_at(y)
@@ -52,7 +74,7 @@
     cross_as = cross_at(1 - y)
     cross_of = 1 - y + cross_as - core
 
-    first = jnp.where(odd, 1, jnp.where(z < 4, 0, 2))
+    first = jnp.where(odd, 1, jnp.where(z == 0, 0, jnp.where(z == 6, 2, 2 * core)))
     right_own = (z + first) % 8 == 0
     second = jnp.where(odd, 2 - 2 * half, 2 - first)
     third = 3 - first - second
@@ -80,6 +102,13 @@
         greet(at(q, z + skew, y, core))
 
     greet(at(q, z - lane, y, core))
+
+    @pl.when(relays)
+    def _():
+        greet(at(q, z - long_lane, y, core))
+        greet(at(q, z - long_lane * (long_way - 2), y, core))
+        greet(at(q, z - long_lane * 2, y, core))
+
     greet(at(q, z, 1 - y, core))
     greet(at(q, z - pass_lane, y, core))
 
@@ -97,7 +126,8 @@
     load_cols.start()
     load.wait()
     load_cols.wait()
-    pl.semaphore_wait(barrier, 8 - left_own.astype(jnp.int32) - right_own.astype(jnp.int32))
+    absent = left_own.astype(jnp.int32) + right_own.astype(jnp.int32)
+    pl.semaphore_wait(barrier, 8 - absent + jnp.where(relays, 3, 0))
 
     def rows(piece):
         return pl.ds(piece * PIECE_ROWS, PIECE_ROWS)
@@ -130,8 +160,16 @@
     def left_skew(piece):
         return to_left(own_part(piece), near_slot(land), 0, piece, at(q, z - skew, y, core))
 
+    def left_long(piece):
+        device = at(q, z + long_lane * (long_way - 2), y, core)
+        return move(own_part(piece), relay.at[piece], 0, piece, relay_sem.at[piece], device)
+
+    def left_relay(piece):
+        return to_left(relay.at[piece], near_slot(1 - land), 10, piece, at(q, z + long_lane * 2, y, core))
+
     def left_next(piece):
-        return to_left(left_part(near_slot(land), piece), near_slot(1 - land), 1, piece, at(q, z + lane, y, core))
+        here, there = near_slot(land_of(piece)), near_slot(1 - land_of(piece))
+        return to_left(left_part(here, piece), there, 1, piece, at(q, z + lane_of(piece), y, core))
 
     def left_cross(piece):
         return to_left(left_part(near_slot(cross_of), piece), cross_slot(cross_as), 2, piece, at(q, z, 1 - y, core))
@@ -177,7 +215,7 @@
             block = right[slot, here, :]
             top = block.astype(jnp.bfloat16)
             rest = (block - top.astype(jnp.float32)).astype(jnp.bfloat16)
-            targets = [right_at[slot, inner, place] for place in range(4)]
+            targets = [right_at[slot, place, inner] for place in range(4)]
             for value, kept in ((top, high), (rest, low)):
                 doubled = []
                 for pair in range(2):
@@ -208,16 +246,16 @@
         def _():
             right_ready(own_slot(index), piece)
 
-    def products(piece):
+    def products(piece, slots, fresh):
         def one(index, carry):
             block_row = piece * PIECE_BLOCKS + index
             here = pl.ds(pl.multiple_of(block_row * BS, BS), BS)
             place = lax.broadcasted_iota(jnp.int32, (BS, 256), 1) // BS
             tops, rests, starts = [], [], []
-            for step in range(STEPS):
+            for step in slots:
                 used = jnp.zeros((BS, 256), jnp.bool_)
                 for slot in range(4):
-                    inner = left_at[step, block_row, slot]
+                    inner = left_at[step, slot, block_row]
                     used = used | (place == jnp.where(inner >= 0, slot, -1))
                     starts.append((step, jnp.maximum(inner, 0)))
                 block = jnp.where(used, left[step, here, :], 0.0)
@@ -232,24 +270,30 @@
                 right_rest = jnp.concatenate([low[step, start, :, lanes] for step, start in starts], axis=0)
                 main = jnp.dot(both, right_top, preferred_element_type=jnp.float32)
                 extra = jnp.dot(top, right_rest, preferred_element_type=jnp.float32)
-                out[here, lanes] = main[:BS] + main[BS:] + extra
+                term = main[:BS] + main[BS:] + extra
+                out[here, lanes] = term if fresh else out[here, lanes] + term
             return carry
 
         lax.fori_loop(0, PIECE_BLOCKS, one, 0)
-        write(piece).start()
 
     def write(piece):
         return pltpu.make_async_copy(out.at[rows(piece)], out_hbm.at[rows(piece)], out_sem.at[piece])
 
-    for piece in ALL:
+    def left_start(piece):
         @pl.when(left_own)
         def _():
             keep_left(piece).start()
 
-        @pl.when(jnp.logical_not(left_own))
+        @pl.when(jnp.logical_not(left_own | takes_long(piece)))
         def _():
             left_skew(piece).start()
 
+        if piece != COLS:
+            @pl.when(takes_long(piece))
+            def _():
+                left_long(piece).start()
+
+    def right_start(piece):
         @pl.when(right_own)
         def _():
             keep_right(piece).start()
@@ -257,6 +301,16 @@
         @pl.when(jnp.logical_not(right_own))
         def _():
             right_skew(piece).start()
+
+    def start_after(start, piece, ahead):
+        place = ALL.index(piece) + ahead
+        if place < len(ALL):
+            start(ALL[place])
+
+    for piece in ALL[:RIGHT_AHEAD]:
+        right_start(piece)
+    for piece in ALL[:LEFT_AHEAD]:
+        left_start(piece)
 
     def right_first(piece):
         @pl.when(right_own)
@@ -295,18 +349,18 @@
 
         @pl.when(jnp.logical_not(left_own))
         def _():
-            left_here(near_slot(land), piece)
+            left_here(near_slot(land_of(piece)), piece)
 
         left_next(piece).start()
 
-        @pl.when(cross_of == land)
+        @pl.when(cross_of == land_of(piece))
         def _():
             left_cross(piece).start()
 
     def left_second(piece):
-        left_here(near_slot(1 - land), piece)
-
-        @pl.when(cross_of != land)
+        left_here(near_slot(1 - land_of(piece)), piece)
+
+        @pl.when(cross_of != land_of(piece))
         def _():
             left_cross(piece).start()
 
@@ -317,42 +371,70 @@
     def left_last(piece):
         left_here(cross_slot(1 - crossed), piece)
 
-    def lagged(stages):
-        for turn in range(len(ALL) + len(stages) - 1):
-            for lag, stage in enumerate(stages):
-                if 0 <= turn - lag < len(ALL):
-                    stage(ALL[turn - lag])
-
-    def landed(piece):
+    def relayed(piece):
+        if piece != COLS:
+            @pl.when(takes_long(piece))
+            def _():
+                move(relay.at[piece], relay.at[piece], 0, piece, relay_sem.at[piece], at(q, z, 1 - y, core)).wait_recv()
+                left_relay(piece).start()
+
+    def right_landed(piece):
         right_first(piece)
-        left_first(piece)
+        start_after(right_start, piece, RIGHT_AHEAD)
         own_ready(first, piece)
 
-    def followed(piece):
+    def right_followed(piece):
         right_second(piece)
         own_ready(second, piece)
 
-    def finished(piece):
+    def right_finished(piece):
         right_third(piece)
-        left_second(piece)
         own_ready(third, piece)
 
-    def shared(piece):
-        left_third(piece)
+    def right_shared(piece):
         for index in range(2):
             right_here(shared_slot(index), piece)
             right_ready(shared_slot(index), piece)
 
-    lagged((landed, followed))
-    lagged((finished, shared))
-    for piece in ALL:
+    def left_landed(piece):
+        left_first(piece)
+        start_after(left_start, piece, LEFT_AHEAD)
+
+    def left_ended(piece):
         left_last(piece)
         if piece == COLS:
             copy = pltpu.make_async_copy(left_cols, left_at, at_sem)
             copy.start()
             copy.wait()
-        else:
-            products(piece)
+
+    def near_products(piece):
+        products(piece, (near_slot(0), near_slot(1)), True)
+
+    def crossed_products(piece):
+        products(piece, (cross_slot(crossed),), False)
+
+    def last_products(piece):
+        products(piece, (cross_slot(1 - crossed),), False)
+        write(piece).start()
+
+    events = []
+    for place, piece in enumerate(ALL):
+        right_turn, left_turn = place * RIGHT_PACE, place + 0.3
+        for lag, stage in enumerate((right_landed, right_followed, right_finished, right_shared)):
+            events.append((right_turn + lag * RIGHT_LAG, stage, piece))
+        for lag, stage in enumerate((relayed, left_landed, left_second, left_third)):
+            events.append((left_turn + (lag - 0.5) * LEFT_LAG, stage, piece))
+        events.append((left_turn + 2.5 * LEFT_LAG + END_LAG, left_ended, piece))
+    ready = max(turn for turn, stage, piece in events if stage is right_shared)
+    at_turn = {(stage, piece): turn for turn, stage, piece in events}
+    cols_turn = at_turn[left_ended, COLS]
+    for place, piece in enumerate(ALL[1:]):
+        least = max(ready, cols_turn) + 0.01 + 0.1 * place
+        events.append((max(least, at_turn[left_second, piece] + 0.01), near_products, piece))
+        events.append((max(least + 0.05, at_turn[left_third, piece] + 0.02), crossed_products, piece))
+        events.append((max(least + 0.1, at_turn[left_ended, piece] + 0.01), last_products, piece))
+    for turn, stage, piece in sorted(events, key=lambda event: event[0]):
+        stage(piece)
 
     for piece in ALL:
         @pl.when(jnp.logical_not(left_own))
@@ -362,6 +444,11 @@
         @pl.when(jnp.logical_not(right_own))
         def _():
             right_skew(piece).wait_send()
+
+        if piece != COLS:
+            @pl.when(takes_long(piece))
+            def _():
+                left_relay(piece).wait_send()
 
         left_next(piece).wait_send()
         left_cross(piece).wait_send()
@@ -386,27 +473,29 @@
         out_specs=pl.BlockSpec(memory_space=pl.ANY),
         scratch_shapes=[
             pltpu.VMEM((1024, 256), jnp.float32),
-            pltpu.VMEM((16, 4), jnp.int32),
+            pltpu.VMEM((4, 16), jnp.int32),
             pltpu.VMEM((4, 1024, 256), jnp.float32),
-            pltpu.VMEM((4, 16, 4), jnp.int32),
+            pltpu.VMEM((4, 4, 16), jnp.int32),
             pltpu.VMEM((5, 1024, 256), jnp.float32),
-            pltpu.VMEM((5, 16, 4), jnp.int32),
+            pltpu.VMEM((5, 4, 16), jnp.int32),
+            pltpu.VMEM((PIECES, PIECE_ROWS, 256), jnp.float32),
             pltpu.VMEM((STEPS, 16, BS, 1024), jnp.bfloat16),
             pltpu.VMEM((STEPS, 16, BS, 1024), jnp.bfloat16),
             pltpu.VMEM((1024, 1024), jnp.float32),
-            pltpu.SMEM((4, 16, 4), jnp.int32),
-            pltpu.SMEM((4, 16, 4), jnp.int32),
+            pltpu.SMEM((4, 4, 16), jnp.int32),
+            pltpu.SMEM((4, 4, 16), jnp.int32),
             pltpu.SemaphoreType.DMA((2,)),
             pltpu.SemaphoreType.DMA((2, count)),
-            pltpu.SemaphoreType.DMA((10, count)),
+            pltpu.SemaphoreType.DMA((11, count)),
             pltpu.SemaphoreType.DMA((4, count)),
             pltpu.SemaphoreType.DMA((5, count)),
+            pltpu.SemaphoreType.DMA((PIECES,)),
             pltpu.SemaphoreType.DMA,
             pltpu.SemaphoreType.DMA((PIECES,)),
         ],
         compiler_params=pltpu.CompilerParams(collective_id=0, has_side_effects=True),
         name="window_square",
-    )(p_cols, p_data)
+    )(p_cols.T, p_data)
 
 
 def solution(mesh):

time: 113 us -> 88.4 us (0.78)
  the two profiles are of different devices: /device:TPU:12 before, /device:TPU:24 now
where the time goes in v1:
time: 88.4 us; the launch traced here: 88.2 us
  Pallas kernels  83.4 us (94%)
  local copies, waits for them, and re-layouts  4.79 us (5%)
    pallas_call x1, Pallas kernels, local(): pl.pallas_call(kernel, out_shape=jax.ShapeDtypeStruct((1024, 1024), jnp.f...  83.4 us
    unnamed x1, local copies, waits for them, and re-layouts  4.79 us

profile of v1, /device:TPU:24, one launch (start us, length us, event | category | flops | bytes accessed | tf_op | source)
XLA Modules:
  0.0 88.2 jit_solution(1747501826562321869)
XLA Ops:
  0.0 83.4 %window_square.1 = f32[1024,1024]{1,0:T(8,128)} custom-call(s32[4,16]{1,0:T(4,128)} %bitcast.1, f32[1024,256]{1,0:T(8,128)} %data_hbm.1), custom_call_target="tpu_custom_call" | custom-call | tf_op jit(solution)/shard_map/window_square/pallas_call | solution.py:469
  83.4 4.8 %copy.4 = f32[1024,1024]{1,0:T(8,128)} copy(f32[1024,1024]{1,0:T(8,128)} %window_square.1) | data formatting | bytes 8388608

commit v2 on v1

--- a/solution.py
+++ b/solution.py
@@ -19,14 +19,15 @@
 RIGHT_LAG = 1.4
 LEFT_LAG = 2.0
 END_LAG = 2.0
+SPACING = 0.1
 ALL = (COLS,) + tuple(range(PIECES))
 MESH = pl.DeviceIdType.MESH
 
 
 def kernel(
     cols_hbm, data_hbm, out_hbm,
-    own, own_cols, left, left_cols, right, right_cols, relay, high, low, out, left_at, right_at,
-    load_sem, keep_sem, send_sem, left_sem, right_sem, relay_sem, at_sem, out_sem,
+    left, left_cols, right, right_cols, relay, high, low, out, left_at, right_at,
+    keep_sem, send_sem, left_sem, right_sem, relay_sem, at_sem, out_sem,
 ):
     row, col = lax.axis_index("row"), lax.axis_index("col")
     q, core = row // 2, row % 2
@@ -120,12 +121,6 @@
     greet(at(q + jnp.where(odd, -2 * hop, hop), z, y, core))
     greet(at(q, z, y, 1 - core))
 
-    load = pltpu.make_async_copy(data_hbm, own, load_sem.at[0])
-    load_cols = pltpu.make_async_copy(cols_hbm, own_cols, load_sem.at[1])
-    load.start()
-    load_cols.start()
-    load.wait()
-    load_cols.wait()
     absent = left_own.astype(jnp.int32) + right_own.astype(jnp.int32)
     pl.semaphore_wait(barrier, 8 - absent + jnp.where(relays, 3, 0))
 
@@ -133,7 +128,7 @@
         return pl.ds(piece * PIECE_ROWS, PIECE_ROWS)
 
     def own_part(piece):
-        return own_cols if piece == COLS else own.at[rows(piece)]
+        return cols_hbm if piece == COLS else data_hbm.at[rows(piece)]
 
     def left_part(slot, piece):
         return left_cols.at[slot] if piece == COLS else left.at[slot, rows(piece)]
@@ -429,7 +424,7 @@
     at_turn = {(stage, piece): turn for turn, stage, piece in events}
     cols_turn = at_turn[left_ended, COLS]
     for place, piece in enumerate(ALL[1:]):
-        least = max(ready, cols_turn) + 0.01 + 0.1 * place
+        least = max(ready, cols_turn) + 0.01 + SPACING * place
         events.append((max(least, at_turn[left_second, piece] + 0.01), near_products, piece))
         events.append((max(least + 0.05, at_turn[left_third, piece] + 0.02), crossed_products, piece))
         events.append((max(least + 0.1, at_turn[left_ended, piece] + 0.01), last_products, piece))
@@ -464,16 +459,38 @@
             write(piece).wait()
 
 
+def deliver_kernel(result_ref, out_ref, sem):
+    copies = []
+    for index in range(8):
+        rows = pl.ds(index * 128, 128)
+        copies.append(pltpu.make_async_copy(result_ref.at[rows], out_ref.at[rows], sem.at[index]))
+        copies[-1].start()
+    for copy in copies:
+        copy.wait()
+
+
+def deliver(result):
+    return pl.pallas_call(
+        deliver_kernel,
+        out_shape=jax.ShapeDtypeStruct(result.shape, result.dtype),
+        in_specs=[pl.BlockSpec(memory_space=pl.ANY)],
+        out_specs=pl.BlockSpec(memory_space=pl.ANY),
+        scratch_shapes=[
+            pltpu.SemaphoreType.DMA((8,)),
+        ],
+        compiler_params=pltpu.CompilerParams(vmem_limit_bytes=16 * 2**20),
+        name="deliver",
+    )(result)
+
+
 def local(p_cols, p_data):
     count = len(ALL)
-    return pl.pallas_call(
+    result = pl.pallas_call(
         kernel,
         out_shape=jax.ShapeDtypeStruct((1024, 1024), jnp.float32),
-        in_specs=[pl.BlockSpec(memory_space=pl.ANY)] * 2,
+        in_specs=[pl.BlockSpec(memory_space=pltpu.HBM)] * 2,
         out_specs=pl.BlockSpec(memory_space=pl.ANY),
         scratch_shapes=[
-            pltpu.VMEM((1024, 256), jnp.float32),
-            pltpu.VMEM((4, 16), jnp.int32),
             pltpu.VMEM((4, 1024, 256), jnp.float32),
             pltpu.VMEM((4, 4, 16), jnp.int32),
             pltpu.VMEM((5, 1024, 256), jnp.float32),
@@ -484,7 +501,6 @@
             pltpu.VMEM((1024, 1024), jnp.float32),
             pltpu.SMEM((4, 4, 16), jnp.int32),
             pltpu.SMEM((4, 4, 16), jnp.int32),
-            pltpu.SemaphoreType.DMA((2,)),
             pltpu.SemaphoreType.DMA((2, count)),
             pltpu.SemaphoreType.DMA((11, count)),
             pltpu.SemaphoreType.DMA((4, count)),
@@ -493,9 +509,12 @@
             pltpu.SemaphoreType.DMA,
             pltpu.SemaphoreType.DMA((PIECES,)),
         ],
-        compiler_params=pltpu.CompilerParams(collective_id=0, has_side_effects=True),
+        compiler_params=pltpu.CompilerParams(
+            collective_id=0, has_side_effects=True, vmem_limit_bytes=36 * 2**20
+        ),
         name="window_square",
     )(p_cols.T, p_data)
+    return deliver(result)
 
 
 def solution(mesh):

time: 88.4 us -> 86.9 us (0.983)
  the two profiles are of different devices: /device:TPU:24 before, /device:TPU:12 now
where the time goes in v2:
time: 86.9 us; the launch traced here: 86.2 us
  Pallas kernels  84.2 us (97%)
  local copies, waits for them, and re-layouts  1.91 us (2%)
    pallas_call x1, Pallas kernels, local(): pl.pallas_call(kernel, out_shape=jax.ShapeDtypeStruct((1024, 1024), jnp.f...  82.1 us
    pallas_call x1, Pallas kernels, deliver(): pl.pallas_call(deliver_kernel, out_shape=jax.ShapeDtypeStruct(result.shap...  2.07 us
    unnamed x4, local copies, waits for them, and re-layouts  1.91 us

profile of v2, /device:TPU:12, one launch (start us, length us, event | category | flops | bytes accessed | tf_op | source)
XLA Modules:
  0.0 86.2 jit_solution(16708399326861094550)
XLA Ops:
  0.0 0.0 copy-start
  0.0 1.2 %copy-done = f32[1024,256]{1,0:T(8,128)S(1)} copy-done((f32[1024,256]{1,0:T(8,128)S(1)}, f32[1024,256]{1,0:T(8,128)}, u32[]{:S(2)}) %copy-start) | copy-done | bytes 1048600
  1.2 0.0 copy-start.1
  1.2 0.7 copy-done.1
  1.9 82.1 %window_square.1.result_ref = f32[1024,1024]{1,0:T(8,128)S(1)} custom-call(s32[4,16]{1,0:T(4,128)S(1)} %bitcast.1, f32[1024,256]{1,0:T(8,128)S(1)} %copy-done), custom_call_target="tpu_custom_call" | custom-call | tf_op jit(solution)/shard_map/window_square/pallas_call | solution.py:488
  84.0 2.1 %deliver.1 = f32[1024,1024]{1,0:T(8,128)} custom-call(f32[1024,1024]{1,0:T(8,128)S(1)} %window_square.1.result_ref), custom_call_target="tpu_custom_call" | custom-call | tf_op jit(solution)/shard_map/deliver/pallas_call | solution.py:473
Async XLA Ops:
  0.0 1.2 %copy-start = (f32[1024,256]{1,0:T(8,128)S(1)}, f32[1024,256]{1,0:T(8,128)}, u32[]{:S(2)}) copy-start(f32[1024,256]{1,0:T(8,128)} %data_hbm.1) | copy-start | bytes 3145732
  1.2 0.7 copy-start.1
